TPU v7x, 32 devices: a whole 2x2x4 slice. The times are simulated.
32 devices in a mesh: dp: 4 (over y, core), lat: 8 (over z, x).
Axes of the slice: x: 2, y: 2, z: 4, core: 2. Of those that a mesh axis runs over, the one named last changes fastest.
Arguments:
- inputs: bfloat16 [4, 96, 180, 768], P('dp', 'lat'), may hold values from -6 to 6
- cotangent: bfloat16 [4, 96, 180, 768], P('dp', 'lat'), may hold values from -6 to 6
- storm_weight: int32 [4], P('dp'), may hold values from 32 to 192
- norm_gain: float32 [768], replicated, may hold values from 0.5 to 1.5
- norm_shift: float32 [768], replicated, may hold values from -1 to 1
- inner_weight: bfloat16 [2, 8, 96, 96], replicated, may hold values from -0.4375 to 0.4375
- inner_bias: float32 [2, 8, 96], replicated, may hold values from -0.1 to 0.1
- outer_weight: bfloat16 [2, 8, 96, 96], replicated, may hold values from -0.4375 to 0.4375
- outer_bias: float32 [2, 8, 96], replicated, may hold values from -0.05 to 0.05
- post_gain: float32 [768], replicated, may hold values from 0.5 to 1.5
- post_shift: float32 [768], replicated, may hold values from -1 to 1
- expand_weight: bfloat16 [768, 3072], replicated, may hold values from -0.21875 to 0.21875
- expand_bias: float32 [3072], replicated, may hold values from -0.5 to 0.5
- reduce_weight: bfloat16 [3072, 768], replicated, may hold values from -0.109375 to 0.109375
- reduce_bias: float32 [768], replicated, may hold values from -0.5 to 0.5
Outputs:
- layer_out: bfloat16 [4, 96, 180, 768], P('dp', 'lat')
- input_grad: float32 [4, 96, 180, 768], P('dp', 'lat')
- norm_gain_grad: float32 [768], replicated
- norm_shift_grad: float32 [768], replicated
- inner_weight_grad: float32 [2, 8, 96, 96], replicated
- inner_bias_grad: float32 [2, 8, 96], replicated
- outer_weight_grad: float32 [2, 8, 96, 96], replicated
- outer_bias_grad: float32 [2, 8, 96], replicated
- post_gain_grad: float32 [768], replicated
- post_shift_grad: float32 [768], replicated
- expand_weight_grad: float32 [768, 3072], replicated
- expand_bias_grad: float32 [3072], replicated
- reduce_weight_grad: float32 [3072, 768], replicated
- reduce_bias_grad: float32 [768], replicated
All inputs are finite; a program needn't handle non-finite values.
Results may differ from a plain program's by a relative error of at most 0.017.
The roundings to bfloat16 on the way count: a program that leaves them out, or rounds other values in their place, can miss the bound.
Values may be sent and summed in bfloat16 or wider, within the bound.
A program may use at most 320 MiB of HBM per device.

v0:
```python
from functools import partial
import math
import jax
import jax.numpy as jnp
from jax import lax
from jax.sharding import PartitionSpec as P

BLOCKS = 8
LAT = 90
LON = 180
LAT_PAD = 96
LON_PAD = 96
shrink_level = 0.01
epsilon = 1e-06


def make_tables():
    mode_ids = jnp.arange(LON_PAD, dtype=jnp.int32)
    columns = jnp.arange(LON, dtype=jnp.int32)
    phases = (columns[:, None] * mode_ids[None, :] % LON).astype(jnp.float32) * (
        2.0 * math.pi / LON
    )
    kept_modes = (mode_ids < LON // 2 + 1).astype(jnp.float32)
    factor = (
        jnp.where((mode_ids == 0) | (mode_ids == LON // 2), 1.0, 2.0).astype(jnp.float32)
        * kept_modes
    )
    scaling = 1.0 / math.sqrt(LON)
    forward_lon = (
        jnp.stack([jnp.cos(phases) * kept_modes, -jnp.sin(phases) * kept_modes], axis=1) * scaling
    )
    inverse_lon = jnp.stack([jnp.cos(phases) * factor, -jnp.sin(phases) * factor], axis=1) * scaling
    row_ids = jnp.arange(LAT_PAD, dtype=jnp.int32)
    angles = (row_ids[:, None] * row_ids[None, :] % LAT).astype(jnp.float32) * (2.0 * math.pi / LAT)
    inside = ((row_ids[:, None] < LAT) & (row_ids[None, :] < LAT)).astype(jnp.float32) / math.sqrt(
        LAT
    )
    cosine = jnp.cos(angles) * inside
    sine_part = jnp.sin(angles) * inside
    forward_lat = jnp.stack(
        [jnp.stack([cosine, sine_part], axis=1), jnp.stack([-sine_part, cosine], axis=1)], axis=0
    )
    inverse_lat = jnp.stack(
        [jnp.stack([cosine, -sine_part], axis=1), jnp.stack([sine_part, cosine], axis=1)], axis=0
    )
    return (
        forward_lon.astype(jnp.bfloat16),
        inverse_lon.astype(jnp.bfloat16),
        forward_lat.astype(jnp.bfloat16),
        inverse_lat.astype(jnp.bfloat16),
    )


def layer_norm(values, gain, shift):
    center = jnp.mean(values, axis=-1, keepdims=True)
    spread = jnp.mean(jnp.square(values - center), axis=-1, keepdims=True)
    return (values - center) * lax.rsqrt(spread + epsilon) * gain + shift


def soft_shrink(values):
    return values - shrink_level * jnp.tanh(values / shrink_level)


def gelu_exact(values):
    return jax.nn.gelu(values, approximate=False)


def split_blocks(spectrum):
    samples, modes_k, _, modes_m, width = spectrum.shape
    block_shape = (samples, modes_k, modes_m, BLOCKS, width // BLOCKS)
    return (spectrum[:, :, 0].reshape(block_shape), spectrum[:, :, 1].reshape(block_shape))


def join_blocks(real, imag):
    samples, modes_k, modes_m, _, _ = real.shape
    flat_shape = (samples, modes_k, modes_m, real.shape[3] * real.shape[4])
    return jnp.stack([real.reshape(flat_shape), imag.reshape(flat_shape)], axis=2)


def complex_mix(real, imag, weight, bias):
    product = partial(jnp.einsum, "skmbi,bio->skmbo", preferred_element_type=jnp.float32)
    return (
        product(real, weight[0]) - product(imag, weight[1]) + bias[0],
        product(imag, weight[0]) + product(real, weight[1]) + bias[1],
    )


def mix_back(real, imag, weight, grad_re, grad_im):
    contract = partial(jnp.einsum, "skmbi,skmbo->bio", preferred_element_type=jnp.float32)
    weight_first = contract(real, grad_re) + contract(imag, grad_im)
    weight_second = contract(real, grad_im) - contract(imag, grad_re)
    bias_grad = jnp.stack(
        [
            jnp.sum(grad_re, axis=(0, 1, 2), dtype=jnp.float32),
            jnp.sum(grad_im, axis=(0, 1, 2), dtype=jnp.float32),
        ],
        axis=0,
    )
    backward = partial(jnp.einsum, "skmbo,bio->skmbi", preferred_element_type=jnp.float32)
    input_re = backward(grad_re, weight[0]) + backward(grad_im, weight[1])
    input_im = backward(grad_im, weight[0]) - backward(grad_re, weight[1])
    return (jnp.stack([weight_first, weight_second], axis=0), bias_grad, input_re, input_im)


def shards(
    inputs,
    cotangent,
    storm_weight,
    norm_gain,
    norm_shift,
    inner_weight,
    inner_bias,
    outer_weight,
    outer_bias,
    post_gain,
    post_shift,
    expand_weight,
    expand_bias,
    reduce_weight,
    reduce_bias,
):
    slab_rows = inputs.shape[1]
    width = inputs.shape[3]
    row_ids = lax.axis_index("lat") * slab_rows + jnp.arange(slab_rows, dtype=jnp.int32)
    row_keep = (row_ids < LAT).astype(jnp.float32)
    forward_lon, inverse_lon, forward_lat, inverse_lat = make_tables()
    values = inputs.astype(jnp.float32)
    first, norm_pull = jax.vjp(layer_norm, values, norm_gain, norm_shift)
    first_low = first.astype(jnp.bfloat16)
    lon_spec = jnp.einsum(
        "srwc,wqm->srqmc", first_low, forward_lon, preferred_element_type=jnp.float32
    ).astype(jnp.bfloat16)
    mode_slab = lax.all_to_all(lon_spec, "lat", split_axis=3, concat_axis=1, tiled=True)
    freq = jnp.einsum(
        "qkpr,srpmc->skqmc", forward_lat, mode_slab, preferred_element_type=jnp.float32
    ).astype(jnp.bfloat16)
    freq_re, freq_im = split_blocks(freq)
    inner_re, inner_im = complex_mix(freq_re, freq_im, inner_weight, inner_bias)
    hidden_re_full, inner_re_pull = jax.vjp(gelu_exact, inner_re)
    hidden_im_full, inner_im_pull = jax.vjp(gelu_exact, inner_im)
    hidden_re = hidden_re_full.astype(jnp.bfloat16)
    hidden_im = hidden_im_full.astype(jnp.bfloat16)
    outer_re, outer_im = complex_mix(hidden_re, hidden_im, outer_weight, outer_bias)
    shrunk_re, outer_re_pull = jax.vjp(soft_shrink, outer_re)
    shrunk_im, outer_im_pull = jax.vjp(soft_shrink, outer_im)
    shrunk = join_blocks(shrunk_re.astype(jnp.bfloat16), shrunk_im.astype(jnp.bfloat16))
    back_slab = jnp.einsum(
        "qrpk,skpmc->srqmc", inverse_lat, shrunk, preferred_element_type=jnp.float32
    ).astype(jnp.bfloat16)
    row_spec = lax.all_to_all(back_slab, "lat", split_axis=1, concat_axis=3, tiled=True)
    filtered = jnp.einsum(
        "wqm,srqmc->srwc", inverse_lon, row_spec, preferred_element_type=jnp.float32
    )
    mixed = filtered + first + values
    second, post_pull = jax.vjp(layer_norm, mixed, post_gain, post_shift)
    second_low = second.astype(jnp.bfloat16).reshape(-1, width)
    pre_act = jnp.dot(second_low, expand_weight, preferred_element_type=jnp.float32) + expand_bias
    activ, gelu_pull = jax.vjp(gelu_exact, pre_act)
    activ_low = activ.astype(jnp.bfloat16)
    branch = jnp.dot(activ_low, reduce_weight, preferred_element_type=jnp.float32) + reduce_bias
    total = mixed + branch.reshape(mixed.shape)
    layer_out = (total * row_keep[None, :, None, None]).astype(jnp.bfloat16)
    sample_scale = storm_weight.astype(jnp.float32) / 64.0
    upstream = (
        cotangent.astype(jnp.float32)
        * sample_scale[:, None, None, None]
        * row_keep[None, :, None, None]
    )
    up_low = upstream.astype(jnp.bfloat16).reshape(-1, width)
    reduce_bias_grad = jnp.sum(up_low, axis=0, dtype=jnp.float32)
    reduce_weight_grad = jnp.dot(activ_low.T, up_low, preferred_element_type=jnp.float32)
    activ_grad = jnp.dot(up_low, reduce_weight.T, preferred_element_type=jnp.float32)
    pre_grad = gelu_pull(activ_grad)[0].astype(jnp.bfloat16)
    expand_bias_grad = jnp.sum(pre_grad, axis=0, dtype=jnp.float32)
    expand_weight_grad = jnp.dot(second_low.T, pre_grad, preferred_element_type=jnp.float32)
    second_grad = jnp.dot(pre_grad, expand_weight.T, preferred_element_type=jnp.float32).reshape(
        mixed.shape
    )
    mixed_norm_grad, post_gain_grad, post_shift_grad = post_pull(second_grad)
    mixed_grad = upstream + mixed_norm_grad
    filt_low = mixed_grad.astype(jnp.bfloat16)
    row_grad = jnp.einsum(
        "wqm,srwc->srqmc", inverse_lon, filt_low, preferred_element_type=jnp.float32
    ).astype(jnp.bfloat16)
    mode_grad = lax.all_to_all(row_grad, "lat", split_axis=3, concat_axis=1, tiled=True)
    merged_grad = jnp.einsum(
        "qrpk,srqmc->skpmc", inverse_lat, mode_grad, preferred_element_type=jnp.float32
    )
    merged_re, merged_im = split_blocks(merged_grad)
    outer_re_grad = outer_re_pull(merged_re)[0].astype(jnp.bfloat16)
    outer_im_grad = outer_im_pull(merged_im)[0].astype(jnp.bfloat16)
    outer_weight_grad, outer_bias_grad, hidden_re_grad, hidden_im_grad = mix_back(
        hidden_re, hidden_im, outer_weight, outer_re_grad, outer_im_grad
    )
    inner_re_grad = inner_re_pull(hidden_re_grad)[0].astype(jnp.bfloat16)
    inner_im_grad = inner_im_pull(hidden_im_grad)[0].astype(jnp.bfloat16)
    inner_weight_grad, inner_bias_grad, freq_re_grad, freq_im_grad = mix_back(
        freq_re, freq_im, inner_weight, inner_re_grad, inner_im_grad
    )
    freq_grad = join_blocks(freq_re_grad.astype(jnp.bfloat16), freq_im_grad.astype(jnp.bfloat16))
    slab_grad = jnp.einsum(
        "qkpr,skqmc->srpmc", forward_lat, freq_grad, preferred_element_type=jnp.float32
    ).astype(jnp.bfloat16)
    lon_grad = lax.all_to_all(slab_grad, "lat", split_axis=1, concat_axis=3, tiled=True)
    first_grad = (
        jnp.einsum("wqm,srqmc->srwc", forward_lon, lon_grad, preferred_element_type=jnp.float32)
        + mixed_grad
    )
    values_grad, norm_gain_grad, norm_shift_grad = norm_pull(first_grad)
    input_grad = values_grad + mixed_grad
    grads = (
        norm_gain_grad,
        norm_shift_grad,
        inner_weight_grad,
        inner_bias_grad,
        outer_weight_grad,
        outer_bias_grad,
        post_gain_grad,
        post_shift_grad,
        expand_weight_grad,
        expand_bias_grad,
        reduce_weight_grad,
        reduce_bias_grad,
    )
    summed = lax.psum(
        (
            grads[0],
            grads[1],
            grads[2],
            grads[3],
            grads[4],
            grads[5],
            grads[6],
            grads[7],
            grads[8],
            grads[9],
            grads[10],
            grads[11],
        ),
        ("dp", "lat"),
    )
    return (
        layer_out,
        input_grad,
        summed[0],
        summed[1],
        summed[2],
        summed[3],
        summed[4],
        summed[5],
        summed[6],
        summed[7],
        summed[8],
        summed[9],
        summed[10],
        summed[11],
    )


def solution(mesh):
    return jax.shard_map(
        shards,
        mesh=mesh,
        in_specs=(
            P("dp", "lat", None, None),
            P("dp", "lat", None, None),
            P("dp"),
            P(),
            P(),
            P(),
            P(),
            P(),
            P(),
            P(),
            P(),
            P(),
            P(),
            P(),
            P(),
        ),
        out_specs=(
            P("dp", "lat", None, None),
            P("dp", "lat", None, None),
            P(),
            P(),
            P(),
            P(),
            P(),
            P(),
            P(),
            P(),
            P(),
            P(),
            P(),
            P(),
        ),
        check_vma=False,
    )
```

profile of v0, /device:TPU:0, one launch (start us, length us, event | category | flops | bytes accessed | tf_op | source)
XLA Modules:
  0.0 1046.6 jit_solution(9826930769798211330)
XLA Ops:
  7.2 2.7 convert_reduce_fusion.1
  14.2 5.4 copy.128
  19.7 7.7 all-to-all-start
  31.0 75.5 %all-to-all-done = bf16[1,12,2,96,768]{4,2,1,0,3:T(2,128)(2,1)S(1)} async-done(((bf16[1,12,2,96,768]{4,2,1,0,3:T(2,128)(2,1)}), bf16[1,12,2,96,768]{4,2,1,0,3:T(2,128)(2,1)S(1)}, u32[]{:S(2)}, u32[]{:S(2)}) %all-to-all-start) | async-done | bytes 3538976 | tf_op jit(solution)/shard_map/all_to_all | solution.py:133
  106.5 3.0 copy.129
  114.7 3.4 reshape.762
  118.2 3.4 copy.160
  121.6 5.5 reshape.763
  127.1 4.6 copy.161
  135.3 11.1 %fusion.115 = (bf16[96,12,8,96]{3,0,1,2:T(8,128)(2,1)S(1)}, f32[1,96,12,8,96]{4,1,2,3,0:T(8,128)}) fusion(f32[8,96,1,96,12]{1,3,4,0,2:T(8,128)S(1)} %bitcast_add_fusion.4), kind=kLoop, calls=%fused_computation.168 | loop fusion | flops 57507840 | bytes 8847360 | tf_op jit(solution)/shard_map/reshape.13
  147.4 11.1 %fusion.116 = (bf16[96,12,8,96]{3,0,1,2:T(8,128)(2,1)S(1)}, f32[1,96,12,8,96]{4,1,2,3,0:T(8,128)}) fusion(f32[8,96,1,96,12]{1,3,4,0,2:T(8,128)S(1)} %bitcast_add_fusion.3), kind=kLoop, calls=%fused_computation.169 | loop fusion | flops 57507840 | bytes 8847360 | tf_op jit(solution)/shard_map/reshape.34
  159.3 2.9 fusion.211
  162.3 3.5 subtract_convert_fusion.2
  165.8 2.9 copy.136
  168.7 4.9 stack_reshape.12
  173.6 5.7 subtract_convert_fusion.1
  180.8 2.9 stack_reshape.13
  183.7 3.1 fusion.70
  186.8 5.4 copy.140
  192.3 5.2 all-to-all-start.1
  198.1 3.7 convert_reduce_fusion.2
  201.8 5.6 reshape.770
  208.5 67.5 %all-to-all-done.1 = bf16[1,96,2,12,768]{4,2,3,0,1:T(2,128)(2,1)} async-done(((bf16[1,96,2,12,768]{4,2,3,0,1:T(2,128)(2,1)}), bf16[1,96,2,12,768]{4,2,3,0,1:T(2,128)(2,1)}, u32[]{:S(2)}, u32[]{:S(2)}) %all-to-all-start.1) | async-done | bytes 3538976 | tf_op jit(solution)/shard_map/all_to_all | solution.py:150
  276.0 5.1 copy.141
  281.2 3.2 fusion.292
  284.4 2.8 copy-done
  289.5 3.6 add_convert_fusion.1
  293.1 3.0 reshape.768
  296.2 70.7 %multiply_convert_fusion = (bf16[2160,3072]{1,0:T(8,128)(2,1)}, f32[2160,3072]{1,0:T(8,128)}, f32[2160,3072]{1,0:T(8,128)}) fusion(f32[3072]{0:T(1024)S(1)} %copy-done.78, bf16[2160,768]{1,0:T(8,128)(2,1)} %reshape.768, bf16[768,3072]{1,0:T(8,128)(2,1)} %param.26), kind=kOutput, calls=%fused_computation.4 | convolution fusion | flops 10630103040 | bytes 74403840 | tf_op jit(solution)/shard_map/dot_general | solution.py:157
  366.9 29.7 %convert_reduce_fusion = (f32[3072]{0:T(1024)}, bf16[2160,3072]{1,0:T(8,128)(2,1)}) fusion(f32[2160,3072]{1,0:T(8,128)} %get-tuple-element.97, bf16[2160,768]{1,0:T(8,128)(2,1)S(1)} %copy-done.27, bf16[3072,768]{1,0:T(8,128)(2,1)} %param.28, f32[2160,3072]{1,0:T(8,128)} %get-tuple-element.131, f32[3072]{0:T(1024)S(1)} %copy-done.78), kind=kOutput, calls=%fused_computation.2 | convolution fusion | flops 10304959488 | bytes 74416128 | tf_op jit(solution)/shard_map/dot_general | solution.py:172
  396.6 16.6 %fusion.285 = (f32[768]{0:T(1024)}, f32[2160]{0:T(1024)S(1)}, f32[2160,768]{1,0:T(8,128)}) fusion(f32[2160]{0:T(1024)S(1)} %copy-done.69, f32[768]{0:T(1024)S(1)} %copy-done.59, bf16[2160,3072]{1,0:T(8,128)(2,1)} %get-tuple-element.139, bf16[768,3072]{1,0:T(8,128)(2,1)S(1)} %copy-done.77), kind=kOutput, calls=%fused_computation.331 | convolution fusion | flops 10198791168 | bytes 24648576 | tf_op jit(solution)/shard_map/dot_general | solution.py:176
  413.2 7.3 reshape.771
  420.5 7.6 multiply_reduce_fusion
  429.7 16.7 %convolution_add_fusion = f32[2160,768]{1,0:T(8,128)} fusion(bf16[2160,3072]{1,0:T(8,128)(2,1)} %get-tuple-element.96, bf16[3072,768]{1,0:T(8,128)(2,1)} %param.28, f32[768]{0:T(1024)S(1)} %copy-done.79), kind=kOutput, calls=%fused_computation.55 | convolution fusion | flops 10193817600 | bytes 24628224 | tf_op jit(solution)/shard_map/dot_general | solution.py:160
  446.4 7.5 reshape.769
  453.9 9.9 add_add_fusion
  463.8 2.8 copy-done.10
  467.9 5.4 copy.143
  473.3 3.7 all-to-all-start.2
  477.0 17.8 %fusion.293 = f32[768,3072]{1,0:T(8,128)} fusion(bf16[2160,768]{1,0:T(8,128)(2,1)} %reshape.768, bf16[2160,3072]{1,0:T(8,128)(2,1)} %get-tuple-element.139), kind=kOutput, calls=%fused_computation.335 | convolution fusion | flops 10192158720 | bytes 26025984 | tf_op jit(solution)/shard_map/dot_general | solution.py:175
  494.8 16.9 %fusion.294 = f32[3072,768]{1,0:T(8,128)} fusion(bf16[2160,3072]{1,0:T(8,128)(2,1)} %get-tuple-element.96, bf16[2160,768]{1,0:T(8,128)(2,1)S(1)} %copy-done.28), kind=kOutput, calls=%fused_computation.336 | convolution fusion | flops 10192158720 | bytes 26025984 | tf_op jit(solution)/shard_map/dot_general | solution.py:171
  511.7 44.5 %all-to-all-done.2 = bf16[1,12,2,96,768]{4,2,1,0,3:T(2,128)(2,1)S(1)} async-done(((bf16[1,12,2,96,768]{4,2,1,0,3:T(2,128)(2,1)}), bf16[1,12,2,96,768]{4,2,1,0,3:T(2,128)(2,1)S(1)}, u32[]{:S(2)}, u32[]{:S(2)}) %all-to-all-start.2) | async-done | bytes 3538976 | tf_op jit(solution)/shard_map/all_to_all | solution.py:185
  556.2 3.0 copy.144
  565.2 3.7 reshape_squeeze.8
  568.9 5.0 convert_reduce_fusion.4
  577.3 5.7 reshape_squeeze.9
  582.9 5.5 convert_reduce_fusion.3
  589.2 3.0 fusion.137
  592.2 4.7 convert_reduce_fusion.6
  604.3 5.5 convert_reduce_fusion.5
  612.9 2.9 copy.152
  615.8 4.7 stack_reshape.14
  626.9 3.1 stack_reshape.15
  630.1 3.1 fusion.71
  633.2 5.4 copy.157
  638.7 4.5 all-to-all-start.3
  643.2 117.1 %all-to-all-done.3 = bf16[1,96,2,12,768]{4,2,3,0,1:T(2,128)(2,1)} async-done(((bf16[1,96,2,12,768]{4,2,3,0,1:T(2,128)(2,1)}), bf16[1,96,2,12,768]{4,2,3,0,1:T(2,128)(2,1)}, u32[]{:S(2)}, u32[]{:S(2)}) %all-to-all-start.3) | async-done | bytes 3538976 | tf_op jit(solution)/shard_map/all_to_all | solution.py:204
  760.3 5.1 copy.158
  765.5 7.1 fusion.19
  776.5 8.1 copy.168
  784.7 41.8 %all-reduce = (f32[768]{0:T(1024)}, f32[768]{0:T(1024)}, f32[2,8,96]{2,1,0:T(8,128)}, f32[2,8,96]{2,1,0:T(8,128)}, f32[768]{0:T(1024)}, /*index=5*/f32[768]{0:T(1024)}, f32[3072]{0:T(1024)}, f32[768]{0:T(1024)}) all-reduce(f32[768]{0:T(1024)S(1)} %get-tuple-element.72, ...), channel_id=1, replica_groups=mesh['dp'=4,'lat'=8] {'dp','lat'}, use_global_device_ids=true, to_apply=%region_11.12 | all-reduce | flops 9984 | bytes 79872 | tf_op jit(solution)/shard_map/psum | solution.py:225
  826.4 196.3 %all-reduce.4.cloned.1.call-done = (f32[2,8,96,96]{3,2,1,0:T(8,128)}, f32[2,8,96,96]{3,2,1,0:T(8,128)}, f32[768,3072]{1,0:T(8,128)}, f32[3072,768]{1,0:T(8,128)}) async-done(((f32[2,8,96,96]{3,2,1,0:T(8,128)}, f32[2,8,96,96]{3,2,1,0:T(8,128)}, f32[768,3072]{1,0:T(8,128)}, f32[3072,768]{1,0:T(8,128)}), (f32[2,8,96,96]{3,2,1,0:T(8,128)}, f32[2,8,96,96]{3,2,1,0:T(8,128)}, f32[768,3072]{1,0:T(8,128)}, ...) | async-done | bytes 20054032 | tf_op jit(solution)/shard_map/psum | solution.py:225
  1027.0 8.8 copy.240
  1035.8 3.7 copy.241
  (245 shorter events, 60.9 us)
Async XLA Ops:
  7.2 4.8 copy-start.64
  7.2 4.7 copy-start.71
  10.2 270.9 %copy-start.33 = (f32[12,180]{1,0:T(8,128)}, f32[12,180]{1,0:T(8,128)S(1)}, u32[]{:S(2)}) copy-start(f32[12,180]{1,0:T(8,128)S(1)} %broadcast_multiply_fusion.1) | copy-start | bytes 25924
  19.7 86.8 %all-to-all-start = ((bf16[1,12,2,96,768]{4,2,1,0,3:T(2,128)(2,1)}), bf16[1,12,2,96,768]{4,2,1,0,3:T(2,128)(2,1)S(1)}, u32[]{:S(2)}, u32[]{:S(2)}) async-start(bf16[1,12,2,96,768]{4,2,1,0,3:T(2,128)(2,1)} %copy.128), calls=%async_computation | async-start | bytes 7077888 | tf_op jit(solution)/shard_map/all_to_all | solution.py:133
  121.5 24.9 %copy-start.1 = (bf16[96,12,8,96]{0,3,1,2:T(8,128)(2,1)}, bf16[96,12,8,96]{0,3,1,2:T(8,128)(2,1)S(1)}, u32[]{:S(2)}) copy-start(bf16[96,12,8,96]{0,3,1,2:T(8,128)(2,1)S(1)} %copy.160) | copy-start | bytes 5308420
  121.6 10.2 copy-start.23
  135.3 11.1 %copy-start.20 = (f32[8,96,1,96,12]{1,3,4,0,2:T(8,128)}, f32[8,96,1,96,12]{1,3,4,0,2:T(8,128)S(1)}, u32[]{:S(2)}) copy-start(f32[8,96,1,96,12]{1,3,4,0,2:T(8,128)S(1)} %bitcast_add_fusion.4) | copy-start | bytes 10616836
  135.3 11.1 %copy-start.62 = (f32[8,96]{1,0:T(8,128)S(1)}, f32[8,96]{1,0:T(8,128)}, u32[]{:S(2)}) copy-start(f32[8,96]{1,0:T(8,128)} %get-tuple-element.117) | copy-start | bytes 9220
  146.4 12.1 %copy-start.11 = (bf16[96,12,8,96]{3,0,1,2:T(8,128)(2,1)}, bf16[96,12,8,96]{3,0,1,2:T(8,128)(2,1)S(1)}, u32[]{:S(2)}) copy-start(bf16[96,12,8,96]{3,0,1,2:T(8,128)(2,1)S(1)} %get-tuple-element.98) | copy-start | bytes 5308420
  147.4 11.1 %copy-start.19 = (f32[8,96,1,96,12]{1,3,4,0,2:T(8,128)}, f32[8,96,1,96,12]{1,3,4,0,2:T(8,128)S(1)}, u32[]{:S(2)}) copy-start(f32[8,96,1,96,12]{1,3,4,0,2:T(8,128)S(1)} %bitcast_add_fusion.3) | copy-start | bytes 10616836
  147.4 11.1 %copy-start.25 = (bf16[2,8,96,96]{3,2,1,0:T(8,128)(2,1)S(1)}, bf16[2,8,96,96]{3,2,1,0:T(8,128)(2,1)}, u32[]{:S(2)}) copy-start(bf16[2,8,96,96]{3,2,1,0:T(8,128)(2,1)} %param.22) | copy-start | bytes 884740
  165.7 7.8 copy-start.12
  165.7 7.8 copy-start.67
  192.3 5.9 copy-start.21
  192.3 83.7 %all-to-all-start.1 = ((bf16[1,96,2,12,768]{4,2,3,0,1:T(2,128)(2,1)}), bf16[1,96,2,12,768]{4,2,3,0,1:T(2,128)(2,1)}, u32[]{:S(2)}, u32[]{:S(2)}) async-start(bf16[1,96,2,12,768]{4,2,3,0,1:T(2,128)(2,1)} %copy.140), calls=%async_computation.1 | async-start | bytes 7077888 | tf_op jit(solution)/shard_map/all_to_all | solution.py:150
  198.1 9.3 copy-start.75
  207.4 73.7 %copy-start.6 = (bf16[1,12,180,768]{3,2,1,0:T(8,128)(2,1)S(1)}, bf16[1,12,180,768]{3,2,1,0:T(8,128)(2,1)}, u32[]{:S(2)}) copy-start(bf16[1,12,180,768]{3,2,1,0:T(8,128)(2,1)} %param.15) | copy-start | bytes 9953284
  207.4 73.7 %copy-start.56 = (f32[12,180]{1,0:T(8,128)S(1)}, f32[12,180]{1,0:T(8,128)}, u32[]{:S(2)}) copy-start(f32[12,180]{1,0:T(8,128)} %copy-done.55) | copy-start | bytes 25924
  207.4 73.7 %copy-start.65 = (f32[768]{0:T(1024)S(1)}, f32[768]{0:T(1024)}, u32[]{:S(2)}) copy-start(f32[768]{0:T(1024)} %param.18) | copy-start | bytes 9220
  207.4 73.7 %copy-start.72 = (f32[768]{0:T(1024)S(1)}, f32[768]{0:T(1024)}, u32[]{:S(2)}) copy-start(f32[768]{0:T(1024)} %param.19) | copy-start | bytes 9220
  208.5 75.8 %copy-start.39 = (f32[180,1,96]{2,0,1:T(8,128)}, f32[180,1,96]{2,0,1:T(8,128)S(1)}, u32[]{:S(2)}) copy-start(f32[180,1,96]{2,0,1:T(8,128)S(1)} %get-tuple-element.118) | copy-start | bytes 207364
  276.0 5.1 copy-start.41
  284.4 5.1 copy-start.58
  284.4 5.1 copy-start.73
  284.4 8.7 copy-start.29
  296.2 70.7 %copy-start.27 = (bf16[2160,768]{1,0:T(8,128)(2,1)S(1)}, bf16[2160,768]{1,0:T(8,128)(2,1)}, u32[]{:S(2)}) copy-start(bf16[2160,768]{1,0:T(8,128)(2,1)} %reshape.770) | copy-start | bytes 9953284
  366.9 29.7 %copy-start.59 = (f32[768]{0:T(1024)S(1)}, f32[768]{0:T(1024)}, u32[]{:S(2)}) copy-start(f32[768]{0:T(1024)} %param.24) | copy-start | bytes 9220
  366.9 29.7 %copy-start.69 = (f32[2160]{0:T(1024)S(1)}, f32[2160]{0:T(1024)}, u32[]{:S(2)}) copy-start(f32[2160]{0:T(1024)} %rsqrt.26) | copy-start | bytes 25924
  366.9 29.7 %copy-start.77 = (bf16[768,3072]{1,0:T(8,128)(2,1)S(1)}, bf16[768,3072]{1,0:T(8,128)(2,1)}, u32[]{:S(2)}) copy-start(bf16[768,3072]{1,0:T(8,128)(2,1)} %param.26) | copy-start | bytes 14155780
  413.2 7.3 copy-start.30
  413.2 7.3 copy-start.32
  413.2 15.0 %slice-start = ((s8[6782976]{0:T(1024)(128)(4,1)}), s8[2588672]{0:T(1024)(128)(4,1)S(1)}, s32[]{:S(2)}) async-start(s8[6782976]{0:T(1024)(128)(4,1)} %bitcast.614), calls=%async_computation.5 | async-start | bytes 5177344
  420.5 7.7 copy-start.54
  420.5 7.7 slice-start.1
  446.4 7.5 copy-start.22
  446.4 7.5 copy-start.76
  453.9 12.7 %copy-start.40 = (f32[180,1,96]{2,0,1:T(8,128)S(1)}, f32[180,1,96]{2,0,1:T(8,128)}, u32[]{:S(2)}) copy-start(f32[180,1,96]{2,0,1:T(8,128)} %copy-done.39) | copy-start | bytes 207364
  453.9 12.7 %copy-start.42 = (f32[180,1,96]{2,0,1:T(8,128)S(1)}, f32[180,1,96]{2,0,1:T(8,128)}, u32[]{:S(2)}) copy-start(f32[180,1,96]{2,0,1:T(8,128)} %get-tuple-element.119) | copy-start | bytes 207364
  473.3 82.9 %all-to-all-start.2 = ((bf16[1,12,2,96,768]{4,2,1,0,3:T(2,128)(2,1)}), bf16[1,12,2,96,768]{4,2,1,0,3:T(2,128)(2,1)S(1)}, u32[]{:S(2)}, u32[]{:S(2)}) async-start(bf16[1,12,2,96,768]{4,2,1,0,3:T(2,128)(2,1)} %copy.143), calls=%async_computation.2 | async-start | bytes 7077888 | tf_op jit(solution)/shard_map/all_to_all | solution.py:185
  477.0 545.8 %all-reduce.4.cloned.1.call-start = ((), (), s32[]{:S(2)}) async-start(), calls=%async_computation.4 | async-start | bytes 40894464 | tf_op jit(solution)/shard_map/psum | solution.py:225
  477.0 17.8 %copy-start.28 = (bf16[2160,768]{1,0:T(8,128)(2,1)S(1)}, bf16[2160,768]{1,0:T(8,128)(2,1)}, u32[]{:S(2)}) copy-start(bf16[2160,768]{1,0:T(8,128)(2,1)} %reshape.770) | copy-start | bytes 9953284
  568.9 5.0 copy-start.13
  582.9 5.5 copy-start.26
  582.9 9.2 slice-start.6
  596.9 15.2 %copy-start.8 = (bf16[1,96,12,8,96]{4,1,2,3,0:T(8,128)(2,1)}, bf16[1,96,12,8,96]{4,1,2,3,0:T(8,128)(2,1)S(1)}, u32[]{:S(2)}) copy-start(bf16[1,96,12,8,96]{4,1,2,3,0:T(8,128)(2,1)S(1)} %get-tuple-element.137) | copy-start | bytes 5308420
  599.4 4.9 slice-start.4
  604.3 5.5 copy-start.24
  638.7 121.7 %all-to-all-start.3 = ((bf16[1,96,2,12,768]{4,2,3,0,1:T(2,128)(2,1)}), bf16[1,96,2,12,768]{4,2,3,0,1:T(2,128)(2,1)}, u32[]{:S(2)}, u32[]{:S(2)}) async-start(bf16[1,96,2,12,768]{4,2,3,0,1:T(2,128)(2,1)} %copy.157), calls=%async_computation.3 | async-start | bytes 7077888 | tf_op jit(solution)/shard_map/all_to_all | solution.py:204
  643.2 122.3 %copy-start.7 = (bf16[1,12,180,768]{3,2,1,0:T(8,128)(2,1)S(1)}, bf16[1,12,180,768]{3,2,1,0:T(8,128)(2,1)}, u32[]{:S(2)}) copy-start(bf16[1,12,180,768]{3,2,1,0:T(8,128)(2,1)} %param.15) | copy-start | bytes 9953284
  643.2 122.3 %copy-start.34 = (f32[12,180]{1,0:T(8,128)S(1)}, f32[12,180]{1,0:T(8,128)}, u32[]{:S(2)}) copy-start(f32[12,180]{1,0:T(8,128)} %copy-done.33) | copy-start | bytes 25924
  643.2 122.3 %copy-start.36 = (f32[180,1,96]{2,0,1:T(8,128)S(1)}, f32[180,1,96]{2,0,1:T(8,128)}, u32[]{:S(2)}) copy-start(f32[180,1,96]{2,0,1:T(8,128)} %copy-done.35) | copy-start | bytes 207364
  643.2 122.3 %copy-start.57 = (f32[12,180]{1,0:T(8,128)S(1)}, f32[12,180]{1,0:T(8,128)}, u32[]{:S(2)}) copy-start(f32[12,180]{1,0:T(8,128)} %copy-done.55) | copy-start | bytes 25924
  643.2 122.3 %copy-start.66 = (f32[768]{0:T(1024)S(1)}, f32[768]{0:T(1024)}, u32[]{:S(2)}) copy-start(f32[768]{0:T(1024)} %param.18) | copy-start | bytes 9220
  760.3 5.1 copy-start.38
  765.4 8.7 slice-start.2
  765.5 7.1 copy-start.52
  765.5 8.6 slice-start.3
  776.4 8.2 copy-start.60
  776.5 8.2 copy-start.61
  776.5 8.2 copy-start.70
  776.5 8.2 copy-start.74
  1024.8 11.0 %slice-start.8 = ((s8[9437184]{0:T(1024)(128)(4,1)}), s8[4194304]{0:T(1024)(128)(4,1)S(1)}, s32[]{:S(2)}) async-start(s8[9437184]{0:T(1024)(128)(4,1)} %bitcast.626), calls=%async_computation.13 | async-start | bytes 8388608
  1027.0 8.8 slice-start.9
  1027.0 8.8 slice-start.10
  (32 other events, 90.3 us)
Sparse Core Ops, SparseCore 0:
  623.1 399.6 all-reduce.3
where the time goes:
time: 1050 us
  waiting for transfers between devices  501 us (48%)
  matrix products  232 us (22%)
  local copies, waits for them, and re-layouts  162 us (15%)
  other arithmetic  72.2 us (7%)
  blocking collectives  41.8 us (4%)
  starting transfers between devices  21.1 us (2%)
  between operations  16.2 us (2%)
    psum x1, waiting for transfers between devices, shards(): lax.psum((grads[0], grads[1], grads[2], grads[3], grads[4], grads[5], gra...  196 us
    all_to_all x1, waiting for transfers between devices, shards(): lax.all_to_all(slab_grad, 'lat', split_axis=1, concat_axis=3, tiled=True)  117 us
    all_to_all x1, waiting for transfers between devices, shards(): lax.all_to_all(lon_spec, 'lat', split_axis=3, concat_axis=1, tiled=True)  75.5 us
    dot_general x1, matrix products, shards(): jnp.dot(second_low, expand_weight, preferred_element_type=jnp.float32)  70.7 us
    all_to_all x1, waiting for transfers between devices, shards(): lax.all_to_all(back_slab, 'lat', split_axis=1, concat_axis=3, tiled=True)  67.5 us
    all_to_all x1, waiting for transfers between devices, shards(): lax.all_to_all(row_grad, 'lat', split_axis=3, concat_axis=1, tiled=True)  44.5 us
    psum x1, blocking collectives, shards(): lax.psum((grads[0], grads[1], grads[2], grads[3], grads[4], grads[5], gra...  41.8 us
    unnamed x187, local copies, waits for them, and re-layouts  37.9 us
  transfers between devices with their start and end apart: 5, of which 5 were waited for; matrix products, arithmetic and copies ran while one was open for 8% of the time, Pallas kernels for 0%

commit v1 on v0

--- a/solution.py
+++ b/solution.py
@@ -223,21 +223,24 @@
         reduce_bias_grad,
     )
     summed = lax.psum(
-        (
-            grads[0],
-            grads[1],
-            grads[2],
-            grads[3],
-            grads[4],
-            grads[5],
-            grads[6],
-            grads[7],
-            grads[8],
-            grads[9],
-            grads[10],
-            grads[11],
+        lax.psum(
+            (
+                grads[0],
+                grads[1],
+                grads[2],
+                grads[3],
+                grads[4],
+                grads[5],
+                grads[6],
+                grads[7],
+                grads[8],
+                grads[9],
+                grads[10],
+                grads[11],
+            ),
+            "lat",
         ),
-        ("dp", "lat"),
+        "dp",
     )
     return (
         layer_out,

time: 1050 us -> 1610 us (1.53)
  waiting for transfers between devices: 501 us -> 1050 us
    psum x1, waiting for transfers between devices: 196 us -> 602 us  [shards(): lax.psum((grads[0], grads[1], grads[2], grads[3], grads[4], grads[5], gra...]
    psum x0 -> x1, waiting for transfers between devices: none -> 177 us  [shards(): lax.psum(lax.psum((grads[0], grads[1], grads[2], grads[3], grads[4], grad...]
    all_to_all x1, waiting for transfers between devices: 117 us -> 79.7 us  [shards(): lax.all_to_all(slab_grad, 'lat', split_axis=1, concat_axis=3, tiled=True)]
    unnamed x187 -> x189, local copies, waits for them, and re-layouts: 37.9 us -> 39.4 us
  transfers between devices with their start and end apart: 5 -> 6, of which waited for: 5 -> 6; matrix products, arithmetic and copies ran while one was open for 8% -> 6% of each run, Pallas kernels for 0% -> 0%
where the time goes in v1:
time: 1610 us; the launch traced here: 1600 us
  waiting for transfers between devices  1050 us (65%)
  matrix products  234 us (15%)
  local copies, waits for them, and re-layouts  163 us (10%)
  other arithmetic  70.9 us (4%)
  blocking collectives  49.3 us (3%)
  starting transfers between devices  21.5 us (1%)
  between operations  16.3 us (1%)
    psum x1, waiting for transfers between devices, shards(): lax.psum((grads[0], grads[1], grads[2], grads[3], grads[4], grads[5], gra...  602 us
    psum x1, waiting for transfers between devices, shards(): lax.psum(lax.psum((grads[0], grads[1], grads[2], grads[3], grads[4], grad...  177 us
    all_to_all x1, waiting for transfers between devices, shards(): lax.all_to_all(slab_grad, 'lat', split_axis=1, concat_axis=3, tiled=True)  79.7 us
    all_to_all x1, waiting for transfers between devices, shards(): lax.all_to_all(lon_spec, 'lat', split_axis=3, concat_axis=1, tiled=True)  75.5 us
    dot_general x1, matrix products, shards(): jnp.dot(second_low, expand_weight, preferred_element_type=jnp.float32)  70.3 us
    all_to_all x1, waiting for transfers between devices, shards(): lax.all_to_all(back_slab, 'lat', split_axis=1, concat_axis=3, tiled=True)  67.5 us
    all_to_all x1, waiting for transfers between devices, shards(): lax.all_to_all(row_grad, 'lat', split_axis=3, concat_axis=1, tiled=True)  44.4 us
    unnamed x189, local copies, waits for them, and re-layouts  39.4 us
  transfers between devices with their start and end apart: 6, of which 6 were waited for; matrix products, arithmetic and copies ran while one was open for 6% of the time, Pallas kernels for 0%

profile of v1, /device:TPU:0, one launch (start us, length us, event | category | flops | bytes accessed | tf_op | source)
XLA Modules:
  0.0 1601.7 jit_solution(8874353259919118157)
XLA Ops:
  14.2 5.4 copy.128
  19.6 7.7 all-to-all-start
  31.0 75.5 %all-to-all-done = bf16[1,12,2,96,768]{4,2,1,0,3:T(2,128)(2,1)S(1)} async-done(((bf16[1,12,2,96,768]{4,2,1,0,3:T(2,128)(2,1)}), bf16[1,12,2,96,768]{4,2,1,0,3:T(2,128)(2,1)S(1)}, u32[]{:S(2)}, u32[]{:S(2)}) %all-to-all-start) | async-done | bytes 3538976 | tf_op jit(solution)/shard_map/all_to_all | solution.py:133
  106.5 3.0 copy.129
  114.7 3.4 reshape.762
  118.1 3.4 copy.160
  121.6 5.5 reshape.763
  127.1 4.6 copy.161
  135.3 11.1 fusion.115
  147.4 11.1 fusion.116
  159.3 2.9 fusion.211
  162.2 3.5 subtract_convert_fusion.2
  165.7 2.9 copy.136
  168.6 4.9 stack_reshape.12
  173.5 5.7 subtract_convert_fusion.1
  180.7 2.9 stack_reshape.13
  183.6 3.1 fusion.70
  186.8 5.4 copy.140
  192.2 5.2 all-to-all-start.1
  198.1 3.7 convert_reduce_fusion.2
  201.8 5.6 reshape.770
  208.5 67.5 %all-to-all-done.1 = bf16[1,96,2,12,768]{4,2,3,0,1:T(2,128)(2,1)} async-done(((bf16[1,96,2,12,768]{4,2,3,0,1:T(2,128)(2,1)}), bf16[1,96,2,12,768]{4,2,3,0,1:T(2,128)(2,1)}, u32[]{:S(2)}, u32[]{:S(2)}) %all-to-all-start.1) | async-done | bytes 3538976 | tf_op jit(solution)/shard_map/all_to_all | solution.py:150
  276.0 5.1 copy.141
  281.1 3.2 fusion.292
  289.4 3.6 add_convert_fusion.1
  293.1 3.0 reshape.768
  296.1 70.3 %multiply_convert_fusion = (bf16[2160,3072]{1,0:T(8,128)(2,1)}, f32[2160,3072]{1,0:T(8,128)}, f32[2160,3072]{1,0:T(8,128)}) fusion(f32[3072]{0:T(1024)S(1)} %copy-done.79, bf16[2160,768]{1,0:T(8,128)(2,1)} %reshape.768, bf16[768,3072]{1,0:T(8,128)(2,1)} %param.26), kind=kOutput, calls=%fused_computation.4 | convolution fusion | flops 10630103040 | bytes 74403840 | tf_op jit(solution)/shard_map/dot_general | solution.py:157
  366.5 29.7 %convert_reduce_fusion = (f32[3072]{0:T(1024)}, bf16[2160,3072]{1,0:T(8,128)(2,1)}) fusion(f32[2160,3072]{1,0:T(8,128)} %get-tuple-element.109, bf16[2160,768]{1,0:T(8,128)(2,1)S(1)} %copy-done.28, bf16[3072,768]{1,0:T(8,128)(2,1)} %param.28, f32[2160,3072]{1,0:T(8,128)} %get-tuple-element.143, f32[3072]{0:T(1024)S(1)} %copy-done.79), kind=kOutput, calls=%fused_computation.2 | convolution fusion | flops 10304959488 | bytes 74416128 | tf_op jit(solution)/shard_map/dot_general | solution.py:172
  396.2 16.6 %fusion.285 = (f32[768]{0:T(1024)}, f32[2160]{0:T(1024)S(1)}, f32[2160,768]{1,0:T(8,128)}) fusion(f32[2160]{0:T(1024)S(1)} %copy-done.70, f32[768]{0:T(1024)S(1)} %copy-done.60, bf16[2160,3072]{1,0:T(8,128)(2,1)} %get-tuple-element.151, bf16[768,3072]{1,0:T(8,128)(2,1)S(1)} %copy-done.78), kind=kOutput, calls=%fused_computation.331 | convolution fusion | flops 10198791168 | bytes 24648576 | tf_op jit(solution)/shard_map/dot_general | solution.py:176
  412.8 7.3 reshape.771
  420.1 7.4 multiply_reduce_fusion
  429.0 16.7 %convolution_add_fusion = f32[2160,768]{1,0:T(8,128)} fusion(bf16[2160,3072]{1,0:T(8,128)(2,1)} %get-tuple-element.108, bf16[3072,768]{1,0:T(8,128)(2,1)} %param.28, f32[768]{0:T(1024)S(1)} %copy-done.80), kind=kOutput, calls=%fused_computation.55 | convolution fusion | flops 10193817600 | bytes 24628224 | tf_op jit(solution)/shard_map/dot_general | solution.py:160
  445.7 7.5 reshape.769
  453.2 9.9 add_add_fusion
  467.1 5.4 copy.143
  472.5 3.7 all-to-all-start.2
  476.3 17.9 %fusion.293 = f32[768,3072]{1,0:T(8,128)} fusion(bf16[2160,768]{1,0:T(8,128)(2,1)} %reshape.768, bf16[2160,3072]{1,0:T(8,128)(2,1)} %get-tuple-element.151), kind=kOutput, calls=%fused_computation.335 | convolution fusion | flops 10192158720 | bytes 26025984 | tf_op jit(solution)/shard_map/dot_general | solution.py:175
  494.2 16.9 %fusion.294 = f32[3072,768]{1,0:T(8,128)} fusion(bf16[2160,3072]{1,0:T(8,128)(2,1)} %get-tuple-element.108, bf16[2160,768]{1,0:T(8,128)(2,1)S(1)} %copy-done.29), kind=kOutput, calls=%fused_computation.336 | convolution fusion | flops 10192158720 | bytes 26025984 | tf_op jit(solution)/shard_map/dot_general | solution.py:171
  511.1 44.4 %all-to-all-done.2 = bf16[1,12,2,96,768]{4,2,1,0,3:T(2,128)(2,1)S(1)} async-done(((bf16[1,12,2,96,768]{4,2,1,0,3:T(2,128)(2,1)}), bf16[1,12,2,96,768]{4,2,1,0,3:T(2,128)(2,1)S(1)}, u32[]{:S(2)}, u32[]{:S(2)}) %all-to-all-start.2) | async-done | bytes 3538976 | tf_op jit(solution)/shard_map/all_to_all | solution.py:185
  555.5 3.0 copy.144
  564.4 3.7 reshape_squeeze.8
  568.1 5.0 convert_reduce_fusion.4
  576.5 5.7 reshape_squeeze.9
  582.2 5.5 convert_reduce_fusion.3
  587.7 2.9 fusion.139
  590.5 3.0 fusion.137
  593.5 5.4 convert_reduce_fusion.6
  604.9 5.3 convert_reduce_fusion.5
  616.4 2.9 copy.152
  619.3 4.7 stack_reshape.14
  624.0 602.3 %all-reduce.7.cloned.1.call-done = (f32[2,8,96,96]{3,2,1,0:T(8,128)}, f32[2,8,96,96]{3,2,1,0:T(8,128)}, f32[768,3072]{1,0:T(8,128)}, f32[3072,768]{1,0:T(8,128)}) async-done(((f32[2,8,96,96]{3,2,1,0:T(8,128)}, f32[2,8,96,96]{3,2,1,0:T(8,128)}, f32[768,3072]{1,0:T(8,128)}, f32[3072,768]{1,0:T(8,128)}), (f32[2,8,96,96]{3,2,1,0:T(8,128)}, f32[2,8,96,96]{3,2,1,0:T(8,128)}, f32[768,3072]{1,0:T(8,128)}, ...) | async-done | bytes 20054032 | tf_op jit(solution)/shard_map/psum | solution.py:226
  1230.3 2.9 stack_reshape.15
  1233.3 3.8 fusion.71
  1237.1 5.4 copy.157
  1242.5 4.7 all-to-all-start.3
  1247.3 79.7 %all-to-all-done.3 = bf16[1,96,2,12,768]{4,2,3,0,1:T(2,128)(2,1)} async-done(((bf16[1,96,2,12,768]{4,2,3,0,1:T(2,128)(2,1)}), bf16[1,96,2,12,768]{4,2,3,0,1:T(2,128)(2,1)}, u32[]{:S(2)}, u32[]{:S(2)}) %all-to-all-start.3) | async-done | bytes 3538976 | tf_op jit(solution)/shard_map/all_to_all | solution.py:204
  1327.0 5.1 copy.158
  1332.1 7.3 fusion.19
  1343.3 8.1 copy.168
  1351.5 35.8 %all-reduce = (f32[768]{0:T(1024)S(1)}, f32[768]{0:T(1024)S(1)}, f32[2,8,96]{2,1,0:T(8,128)S(1)}, f32[2,8,96]{2,1,0:T(8,128)S(1)}, f32[768]{0:T(1024)S(1)}, /*in...) all-reduce(f32[768]{0:T(1024)S(1)} %get-tuple-element.72, ...), channel_id=1, replica_groups=mesh['dp'=4,'lat'=8] {'lat'}, use_global_device_ids=true, to_apply=%region_11.12 | all-reduce | flops 9984 | bytes 79872 | tf_op jit(solution)/shard_map/psum | solution.py:226
  1387.3 13.5 all-reduce.2
  1400.8 177.0 %all-reduce.9.cloned.1.call-done = (f32[2,8,96,96]{3,2,1,0:T(8,128)}, f32[2,8,96,96]{3,2,1,0:T(8,128)}, f32[768,3072]{1,0:T(8,128)}, f32[3072,768]{1,0:T(8,128)}) async-done(((f32[2,8,96,96]{3,2,1,0:T(8,128)}, f32[2,8,96,96]{3,2,1,0:T(8,128)}, f32[768,3072]{1,0:T(8,128)}, f32[3072,768]{1,0:T(8,128)}), (f32[2,8,96,96]{3,2,1,0:T(8,128)}, f32[2,8,96,96]{3,2,1,0:T(8,128)}, f32[768,3072]{1,0:T(8,128)}, ...) | async-done | bytes 20054032 | tf_op jit(solution)/shard_map/psum | solution.py:225
  1582.1 8.8 copy.244
  1590.9 3.7 copy.245
  (251 shorter events, 67.5 us)
Async XLA Ops:
  7.2 4.7 copy-start.65
  7.2 4.7 copy-start.72
  10.2 270.9 %copy-start.34 = (f32[12,180]{1,0:T(8,128)}, f32[12,180]{1,0:T(8,128)S(1)}, u32[]{:S(2)}) copy-start(f32[12,180]{1,0:T(8,128)S(1)} %broadcast_multiply_fusion.1) | copy-start | bytes 25924
  19.6 86.8 %all-to-all-start = ((bf16[1,12,2,96,768]{4,2,1,0,3:T(2,128)(2,1)}), bf16[1,12,2,96,768]{4,2,1,0,3:T(2,128)(2,1)S(1)}, u32[]{:S(2)}, u32[]{:S(2)}) async-start(bf16[1,12,2,96,768]{4,2,1,0,3:T(2,128)(2,1)} %copy.128), calls=%async_computation | async-start | bytes 7077888 | tf_op jit(solution)/shard_map/all_to_all | solution.py:133
  121.5 24.9 %copy-start.1 = (bf16[96,12,8,96]{0,3,1,2:T(8,128)(2,1)}, bf16[96,12,8,96]{0,3,1,2:T(8,128)(2,1)S(1)}, u32[]{:S(2)}) copy-start(bf16[96,12,8,96]{0,3,1,2:T(8,128)(2,1)S(1)} %copy.160) | copy-start | bytes 5308420
  121.6 10.1 copy-start.24
  135.3 11.1 copy-start.21
  135.3 11.1 copy-start.63
  146.4 12.1 copy-start.12
  147.4 11.1 copy-start.20
  147.4 11.1 copy-start.26
  165.7 7.8 copy-start.13
  165.7 7.8 copy-start.68
  192.2 5.9 copy-start.22
  192.2 83.8 %all-to-all-start.1 = ((bf16[1,96,2,12,768]{4,2,3,0,1:T(2,128)(2,1)}), bf16[1,96,2,12,768]{4,2,3,0,1:T(2,128)(2,1)}, u32[]{:S(2)}, u32[]{:S(2)}) async-start(bf16[1,96,2,12,768]{4,2,3,0,1:T(2,128)(2,1)} %copy.140), calls=%async_computation.1 | async-start | bytes 7077888 | tf_op jit(solution)/shard_map/all_to_all | solution.py:150
  198.0 9.3 copy-start.76
  207.3 73.7 %copy-start.6 = (bf16[1,12,180,768]{3,2,1,0:T(8,128)(2,1)S(1)}, bf16[1,12,180,768]{3,2,1,0:T(8,128)(2,1)}, u32[]{:S(2)}) copy-start(bf16[1,12,180,768]{3,2,1,0:T(8,128)(2,1)} %param.15) | copy-start | bytes 9953284
  207.4 73.7 %copy-start.57 = (f32[12,180]{1,0:T(8,128)S(1)}, f32[12,180]{1,0:T(8,128)}, u32[]{:S(2)}) copy-start(f32[12,180]{1,0:T(8,128)} %copy-done.56) | copy-start | bytes 25924
  207.4 73.7 %copy-start.66 = (f32[768]{0:T(1024)S(1)}, f32[768]{0:T(1024)}, u32[]{:S(2)}) copy-start(f32[768]{0:T(1024)} %param.18) | copy-start | bytes 9220
  207.4 73.7 %copy-start.73 = (f32[768]{0:T(1024)S(1)}, f32[768]{0:T(1024)}, u32[]{:S(2)}) copy-start(f32[768]{0:T(1024)} %param.19) | copy-start | bytes 9220
  208.5 75.8 %copy-start.40 = (f32[180,1,96]{2,0,1:T(8,128)}, f32[180,1,96]{2,0,1:T(8,128)S(1)}, u32[]{:S(2)}) copy-start(f32[180,1,96]{2,0,1:T(8,128)S(1)} %get-tuple-element.130) | copy-start | bytes 207364
  276.0 5.1 copy-start.42
  284.3 5.1 copy-start.59
  284.3 5.1 copy-start.74
  284.3 8.7 copy-start.30
  296.1 70.3 %copy-start.28 = (bf16[2160,768]{1,0:T(8,128)(2,1)S(1)}, bf16[2160,768]{1,0:T(8,128)(2,1)}, u32[]{:S(2)}) copy-start(bf16[2160,768]{1,0:T(8,128)(2,1)} %reshape.770) | copy-start | bytes 9953284
  366.4 29.7 %copy-start.60 = (f32[768]{0:T(1024)S(1)}, f32[768]{0:T(1024)}, u32[]{:S(2)}) copy-start(f32[768]{0:T(1024)} %param.24) | copy-start | bytes 9220
  366.4 29.7 %copy-start.70 = (f32[2160]{0:T(1024)S(1)}, f32[2160]{0:T(1024)}, u32[]{:S(2)}) copy-start(f32[2160]{0:T(1024)} %rsqrt.26) | copy-start | bytes 25924
  366.5 29.7 %copy-start.78 = (bf16[768,3072]{1,0:T(8,128)(2,1)S(1)}, bf16[768,3072]{1,0:T(8,128)(2,1)}, u32[]{:S(2)}) copy-start(bf16[768,3072]{1,0:T(8,128)(2,1)} %param.26) | copy-start | bytes 14155780
  412.8 7.3 copy-start.31
  412.8 7.3 copy-start.33
  412.8 14.7 slice-start
  420.1 7.4 copy-start.55
  420.1 7.4 slice-start.1
  445.7 7.5 copy-start.23
  445.7 7.5 copy-start.77
  453.2 12.7 copy-start.41
  453.2 12.6 copy-start.43
  472.5 82.9 %all-to-all-start.2 = ((bf16[1,12,2,96,768]{4,2,1,0,3:T(2,128)(2,1)}), bf16[1,12,2,96,768]{4,2,1,0,3:T(2,128)(2,1)S(1)}, u32[]{:S(2)}, u32[]{:S(2)}) async-start(bf16[1,12,2,96,768]{4,2,1,0,3:T(2,128)(2,1)} %copy.143), calls=%async_computation.2 | async-start | bytes 7077888 | tf_op jit(solution)/shard_map/all_to_all | solution.py:185
  476.2 750.1 %all-reduce.7.cloned.1.call-start = ((), (), s32[]{:S(2)}) async-start(), calls=%async_computation.4 | async-start | bytes 40894464 | tf_op jit(solution)/shard_map/psum | solution.py:226
  476.3 17.9 %copy-start.29 = (bf16[2160,768]{1,0:T(8,128)(2,1)S(1)}, bf16[2160,768]{1,0:T(8,128)(2,1)}, u32[]{:S(2)}) copy-start(bf16[2160,768]{1,0:T(8,128)(2,1)} %reshape.770) | copy-start | bytes 9953284
  568.1 5.0 copy-start.14
  582.2 5.5 copy-start.27
  582.2 11.3 slice-start.6
  587.6 5.8 slice-start.7
  593.5 5.4 copy-start.2
  612.9 964.9 %all-reduce.9.cloned.1.call-start = ((), (), s32[]{:S(2)}) async-start(), calls=%async_computation.5 | async-start | bytes 40894464 | tf_op jit(solution)/shard_map/psum | solution.py:225
  1242.5 84.5 %all-to-all-start.3 = ((bf16[1,96,2,12,768]{4,2,3,0,1:T(2,128)(2,1)}), bf16[1,96,2,12,768]{4,2,3,0,1:T(2,128)(2,1)}, u32[]{:S(2)}, u32[]{:S(2)}) async-start(bf16[1,96,2,12,768]{4,2,3,0,1:T(2,128)(2,1)} %copy.157), calls=%async_computation.3 | async-start | bytes 7077888 | tf_op jit(solution)/shard_map/all_to_all | solution.py:204
  1247.2 84.9 %copy-start.7 = (bf16[1,12,180,768]{3,2,1,0:T(8,128)(2,1)S(1)}, bf16[1,12,180,768]{3,2,1,0:T(8,128)(2,1)}, u32[]{:S(2)}) copy-start(bf16[1,12,180,768]{3,2,1,0:T(8,128)(2,1)} %param.15) | copy-start | bytes 9953284
  1247.2 84.8 %copy-start.35 = (f32[12,180]{1,0:T(8,128)S(1)}, f32[12,180]{1,0:T(8,128)}, u32[]{:S(2)}) copy-start(f32[12,180]{1,0:T(8,128)} %copy-done.34) | copy-start | bytes 25924
  1247.2 84.8 %copy-start.37 = (f32[180,1,96]{2,0,1:T(8,128)S(1)}, f32[180,1,96]{2,0,1:T(8,128)}, u32[]{:S(2)}) copy-start(f32[180,1,96]{2,0,1:T(8,128)} %copy-done.36) | copy-start | bytes 207364
  1247.2 84.8 %copy-start.58 = (f32[12,180]{1,0:T(8,128)S(1)}, f32[12,180]{1,0:T(8,128)}, u32[]{:S(2)}) copy-start(f32[12,180]{1,0:T(8,128)} %copy-done.56) | copy-start | bytes 25924
  1247.2 84.8 %copy-start.67 = (f32[768]{0:T(1024)S(1)}, f32[768]{0:T(1024)}, u32[]{:S(2)}) copy-start(f32[768]{0:T(1024)} %param.18) | copy-start | bytes 9220
  1327.0 5.1 copy-start.39
  1332.0 8.9 slice-start.2
  1332.1 7.3 copy-start.53
  1332.1 8.9 slice-start.3
  1343.3 8.2 copy-start.61
  1343.3 8.2 copy-start.62
  1343.3 8.2 copy-start.71
  1343.3 8.2 copy-start.75
  1579.9 11.0 slice-start.8
  1582.1 8.8 slice-start.9
  1582.1 8.8 slice-start.10
  (34 other events, 89.1 us)
Sparse Core Ops, SparseCore 0:
  613.1 613.1 all-reduce.6
  1229.1 348.6 all-reduce.8
